TPU v7x, 32 devices: a whole 2x2x4 slice. The times are simulated.
32 devices in a mesh: groups: 2 (over y), brick: 4 (over z), ray: 4 (over x, core).
Axes of the slice: x: 2, y: 2, z: 4, core: 2. Of those that a mesh axis runs over, the one named last changes fastest.
Arguments:
- samples_in: bfloat16 [2048, 4, 32, 128], P(('groups', 'ray'), 'brick'), parts along dimension 0, may hold values from -6 to 6
- sample_count: int32 [2048, 4], P(('groups', 'ray'), 'brick'), parts along dimension 0, may hold values from 0 to 32, as said below
- step_length: float32 [2048], P(('groups', 'ray')), parts along dimension 0, may hold values from 0.001 to 0.008
- view_flip: int32 [2048], P(('groups', 'ray')), parts along dimension 0, may hold values 0 or 1
- pixel_grad: float32 [64, 2048], P(None, ('groups', 'ray')), parts along dimension 1, may hold values from -6 to 6
- w_first: bfloat16 [4, 128, 128], P('brick'), may hold values from -0.5 to 0.5
- w_second: bfloat16 [4, 128, 128], P('brick'), may hold values from -0.5 to 0.5
- w_feature: bfloat16 [4, 128, 64], P('brick'), may hold values from -0.5 to 0.5
- w_density: bfloat16 [4, 128], P('brick'), may hold values from -0.5 to 0.5
Outputs:
- grad_samples: bfloat16 [2048, 4, 32, 128], P(('groups', 'ray'), 'brick'), parts along dimension 0
- grad_first: float32 [8, 128, 128], P(('groups', 'brick'), 'ray'), parts along dimension 0
- grad_second: float32 [8, 128, 128], P(('groups', 'brick'), 'ray'), parts along dimension 0
- grad_feature: float32 [8, 128, 64], P(('groups', 'brick'), 'ray'), parts along dimension 0
- grad_density: float32 [8, 128], P(('groups', 'brick'), 'ray'), parts along dimension 0
There are 2 independent parts, one for each index of `groups`. A program takes and returns all parts, laid end to end along the dimension named above; an argument that names none is the same for every part. Nothing has to cross between parts.
Inputs may be any that keep to these rules, and one draw needn't show every extreme that they name: A ray's samples inside a brick are the first sample_count of its block.
All inputs are finite; a program needn't handle non-finite values. No bound on the sum of `view_flip` on one device may be relied on, other than what follows from the above.
Results may differ from a plain program's by a relative error of at most 0.0045.
The roundings to bfloat16 on the way count: a program that leaves them out, or rounds other values in their place, can miss the bound.
Values sent between devices are 32-bit elements; how exact they have to be, the bound alone decides.
A program may use at most 64 MiB of HBM per device.

v0:
```python
import functools

import jax
import jax.numpy as jnp
from jax import lax
from jax.experimental import pallas as pl
from jax.experimental.pallas import tpu as pltpu
from jax.sharding import PartitionSpec as P

LOSS_SCALE = 1024.0
LANES = 256
UNROLL_FORWARD = 1
UNROLL_BACK = 1
PIECES = 8
F32 = jnp.float32
BF16 = jnp.bfloat16
MESH = pl.DeviceIdType.MESH


def iota(shape, dim):
    return lax.broadcasted_iota(jnp.int32, shape, dim)


def split_two(v):
    hi = v.astype(BF16).astype(F32)
    return hi, v - hi


def dot_exact(v, m):
    rows = v.shape[0]
    hi, rest = split_two(v)
    mid, low = split_two(rest)
    out = jnp.dot(
        jnp.concatenate([hi, mid, low], axis=0).astype(BF16), m, preferred_element_type=F32
    )
    return out[:rows] + out[rows : 2 * rows] + out[2 * rows :]


def block_diag(w):
    z = jnp.zeros_like(w)
    return jnp.concatenate(
        [jnp.concatenate([w, z], axis=1), jnp.concatenate([z, w], axis=1)], axis=0
    )


def side(v, right):
    z = jnp.zeros_like(v)
    return jnp.concatenate([z, v] if right else [v, z], axis=1)


def silu_pair(half):
    t = jnp.tanh(half)
    a = 1.0 + t
    h = half * a
    slope = a + h * (1.0 - t)
    return h, slope


def kernel(
    n_brick,
    n_ray,
    per_ray,
    x_hbm,
    count_ref,
    step_ref,
    flip_ref,
    pg_ref,
    w1_ref,
    w2_ref,
    wf_ref,
    wd_ref,
    o_hbm,
    g1_ref,
    g2_ref,
    g3_ref,
    g4_ref,
    x_ref,
    o_ref,
    h1_ref,
    h2_ref,
    xt_ref,
    h1t_ref,
    h2t_ref,
    pre1_even,
    pre1_odd,
    pre2_even,
    pre2_odd,
    s1_ref,
    s2_ref,
    p1_ref,
    p2_ref,
    fg_ref,
    v_ref,
    sc_ref,
    q_ref,
    lg_ref,
    c_ref,
    w1f,
    w2f,
    w1b,
    w2b,
    wfb,
    acc,
    ex_ref,
    red_ref,
    in_sem,
    out_sem,
    ex_send,
    ex_recv,
    red_send,
    red_recv,
):
    rows, width = x_ref.shape
    rays = pg_ref.shape[1]
    feat = pg_ref.shape[0]
    group = LANES // per_ray
    tiles = rows // LANES
    pairs = tiles // 2
    span = 2 * LANES

    x_copy = pltpu.make_async_copy(x_hbm, x_ref, in_sem)
    x_copy.start()

    def out_copy(p):
        at = pl.ds(pl.multiple_of(p * span, span), span)
        return pltpu.make_async_copy(o_ref.at[at], o_hbm.at[at], out_sem.at[p])

    my_brick = lax.axis_index("brick")
    my_ray = lax.axis_index("ray")
    barrier = pltpu.get_barrier_semaphore()
    for d in range(1, n_brick):
        pl.semaphore_signal(
            barrier, inc=1, device_id={"brick": lax.rem(my_brick + d, n_brick)}, device_id_type=MESH
        )
    for d in range(1, n_ray):
        pl.semaphore_signal(
            barrier, inc=1, device_id={"ray": lax.rem(my_ray + d, n_ray)}, device_id_type=MESH
        )

    w1 = w1_ref[0].astype(F32)
    w2 = w2_ref[0].astype(F32)
    wf = wf_ref[0].astype(F32)
    wd = wd_ref[...].astype(F32)
    w1f[...] = block_diag(w1 * 0.5).astype(BF16)
    w2f[...] = block_diag(w2 * 0.5).astype(BF16)
    wide = jnp.concatenate(
        [wf, wd, jnp.zeros((width - feat - 1, width), F32)], axis=0
    )
    wfb[...] = block_diag(wide * 0.5).astype(BF16)
    scaled = jnp.concatenate(
        [LOSS_SCALE * pg_ref[...], jnp.zeros((width - feat, rays), F32)], axis=0
    ).T
    sc_ref[...] = scaled
    v_ref[...] = dot_exact(scaled, wide.astype(BF16))
    acc[...] = jnp.zeros_like(acc)
    group_mask = (iota((group, LANES), 0) == iota((group, LANES), 1) // per_ray).astype(F32)
    wd_rows = jnp.broadcast_to(wd, (8, width))

    pre1 = (pre1_even, pre1_odd)
    pre2 = (pre2_even, pre2_odd)

    def first_layer(p, u):
        at_a = pl.ds(pl.multiple_of(p * span, span), LANES)
        at_b = pl.ds(pl.multiple_of(p * span + LANES, LANES), LANES)
        x = jnp.concatenate([x_ref[at_a, :], x_ref[at_b, :]], axis=1)
        pre1[u][...] = jnp.dot(x, w1f[...], preferred_element_type=F32)

    def first_act(p, u):
        h1, s1 = silu_pair(pre1[u][...])
        h1 = h1.astype(BF16)
        h1_ref[p] = h1
        h1t_ref[p] = h1.T
        s1_ref[p] = s1

    def second_layer(p, u):
        pre2[u][...] = jnp.dot(h1_ref[p], w2f[...], preferred_element_type=F32)

    def second_act(p, u):
        h2, s2 = silu_pair(pre2[u][...])
        h2 = h2.astype(BF16)
        h2_ref[p] = h2
        h2t_ref[p] = h2.T
        s2_ref[p] = s2

    def heads(p):
        left = []
        for k in range(2):
            hi, low = split_two(v_ref[pl.ds(pl.multiple_of((2 * p + k) * group, group), group), :])
            left += [side(hi, k), side(low, k), side(wd_rows, k)]
        left = jnp.concatenate(left, axis=0).astype(BF16)
        got = lax.dot_general(left, h2_ref[p], (((1,), (1,)), ((), ())), preferred_element_type=F32)
        for k in range(2):
            base = k * (2 * group + 8)
            dots = got[base : base + group] + got[base + group : base + 2 * group]
            q_ref[pl.ds(2 * p + k, 1), :] = jnp.sum(dots * group_mask, axis=0, keepdims=True)
            lg_ref[pl.ds(2 * p + k, 1), :] = got[base + 2 * group : base + 2 * group + 1]

    stages = (
        (4, lambda p, u: heads(p)),
        (3, second_act),
        (2, second_layer),
        (1, first_act),
        (0, first_layer),
    )

    def forward_step(p, u, static):
        for back, stage in stages:
            if not static or 0 <= p - back < pairs:
                stage(p - back, (u - back) % 2)

    def forward(i, carry):
        for u in range(2):
            forward_step(2 * i + u, u, False)
        return carry

    x_copy.wait()
    for p in range(4):
        forward_step(p, p % 2, True)
    lax.fori_loop(2, pairs // 2, forward, 0)
    for p in range(pairs, pairs + 4):
        forward_step(p, p % 2, True)

    spread = (iota((rays, LANES), 0) % group == iota((rays, LANES), 1) // per_ray).astype(BF16)
    gather = (iota((LANES, rays), 1) % group == iota((LANES, rays), 0) // per_ray).astype(BF16)
    owner = (iota((tiles, rays), 1) // group == iota((tiles, rays), 0)).astype(F32)
    from_s, to_s = iota((LANES, LANES), 0), iota((LANES, LANES), 1)
    same = from_s // per_ray == to_s // per_ray
    upto = (same & (from_s <= to_s)).astype(BF16)
    later = (same & (from_s > to_s)).astype(BF16)

    def to_samples(*ray_rows):
        out = dot_exact(jnp.concatenate([owner * r for r in ray_rows], axis=0), spread)
        return [out[i * tiles : (i + 1) * tiles] for i in range(len(ray_rows))]

    def to_rays(*sample_values):
        out = dot_exact(jnp.concatenate(sample_values, axis=0), gather)
        return [
            jnp.sum(out[i * tiles : (i + 1) * tiles] * owner, axis=0, keepdims=True)
            for i in range(len(sample_values))
        ]

    logits = lg_ref[...]
    q = q_ref[...]
    count, length = to_samples(count_ref[...].astype(F32), step_ref[...])
    is_valid = (iota((tiles, LANES), 1) % per_ray).astype(F32) < count
    softplus = jnp.maximum(logits, 0.0) + jnp.log1p(jnp.exp(-jnp.abs(logits)))
    depth_step = jnp.where(is_valid, softplus * length, 0.0)
    depth_incl = dot_exact(depth_step, upto)
    half_step = jnp.tanh(0.5 * depth_step)
    weights = jnp.exp(depth_step - depth_incl) * (2.0 * half_step / (1.0 + half_step))
    brick_depth, brick_dot = to_rays(depth_step, weights * q)
    ex_ref[0] = jnp.concatenate([brick_depth, brick_dot, jnp.zeros((6, rays), F32)], axis=0)

    pl.semaphore_wait(barrier, n_brick + n_ray - 2)

    def ex_copy(d):
        return pltpu.make_async_remote_copy(
            src_ref=ex_ref.at[0],
            dst_ref=ex_ref.at[d],
            send_sem=ex_send.at[d],
            recv_sem=ex_recv.at[d],
            device_id={"brick": lax.rem(my_brick + d, n_brick)},
            device_id_type=MESH,
        )

    for d in range(1, n_brick):
        ex_copy(d).start()

    def turn(p, carry):
        at_a = pl.ds(pl.multiple_of(p * span, span), LANES)
        at_b = pl.ds(pl.multiple_of(p * span + LANES, LANES), LANES)
        xt_ref[p] = jnp.concatenate([x_ref[at_a, :], x_ref[at_b, :]], axis=1).T
        return carry

    lax.fori_loop(0, pairs, turn, 0)
    w1b[...] = block_diag(w1_ref[0].astype(F32).T).astype(BF16)
    w2b[...] = block_diag(w2_ref[0].astype(F32).T * 0.5).astype(BF16)
    for d in range(1, n_brick):
        ex_copy(d).wait()

    def walk(order, is_past):
        gap = jnp.zeros((1, rays), F32)
        seen = jnp.zeros((1, rays), F32)
        for k in order:
            there = ex_ref[lax.rem(my_brick - k + n_brick, n_brick)]
            past = jnp.where(is_past(k), 1.0, 0.0)
            seen = seen + past * jnp.exp(-gap) * there[1:2]
            gap = gap + past * there[0:1]
        return gap, seen

    upper_depth, upper_seen = walk(range(n_brick), lambda k: k > my_brick)
    lower_depth, lower_seen = walk(range(n_brick - 1, -1, -1), lambda k: k < my_brick)
    flipped = flip_ref[...] > 0
    through_front = jnp.exp(-jnp.where(flipped, upper_depth, lower_depth))
    behind = jnp.where(flipped, lower_seen, upper_seen)
    front, brick_grad = to_samples(through_front, -through_front * jnp.exp(-brick_depth) * behind)
    own_grad = front * q
    later_sum = dot_exact(weights * own_grad, later)
    step_grad = jnp.exp(-depth_incl) * own_grad - later_sum + brick_grad
    sigmoid = 0.5 + 0.5 * jnp.tanh(0.5 * logits)
    lg_ref[...] = jnp.where(is_valid, step_grad * length * sigmoid, 0.0)
    c_ref[...] = front * weights

    unit = (iota((8, width), 1) == feat).astype(F32)

    def rows_of(pair):
        return jnp.concatenate([pair[:, :width], pair[:, width:]], axis=0)

    def contract_rows(left, right):
        return lax.dot_general(left, right, (((0,), (0,)), ((), ())), preferred_element_type=F32)

    def side_by_side(p):
        left, right = [], []
        for k in range(2):
            t = 2 * p + k
            c_hi, c_low = split_two(c_ref[pl.ds(t, 1), :] * group_mask)
            s_hi, s_low = split_two(sc_ref[pl.ds(pl.multiple_of(t * group, group), group), :])
            left += [c_hi, c_hi, c_low, lg_ref[pl.ds(t, 1), :] * group_mask]
            right += [side(s_hi, k), side(s_low, k), side(s_hi, k), side(unit, k)]
        return jnp.concatenate(left, axis=0).astype(BF16), jnp.concatenate(right, axis=0).astype(BF16)

    def halves_dot(left, right):
        return jnp.dot(left[:width], right[:, :width], preferred_element_type=F32) + jnp.dot(
            left[width:], right[:, width:], preferred_element_type=F32
        )

    def second_grads(p):
        acc[1] += halves_dot(h1t_ref[p], p2_ref[p])
        acc[2] += halves_dot(h2t_ref[p], fg_ref[p])

    def feature_grads(p):
        left, right = side_by_side(p)
        fg_ref[p] = contract_rows(left, right).astype(BF16)

    def back_two(p):
        h2g = jnp.dot(fg_ref[p], wfb[...], preferred_element_type=F32)
        p2_ref[p] = (h2g * s2_ref[p]).astype(BF16)

    def first_grads(p):
        acc[0] += halves_dot(xt_ref[p], p1_ref[p])

    def back_one(p):
        h1g = jnp.dot(p2_ref[p], w2b[...], preferred_element_type=F32)
        p1_ref[p] = (h1g * s1_ref[p]).astype(BF16)

    def pipelined(*stages):
        last = len(stages) - 1

        def step(p, static):
            for back in range(last, -1, -1):
                if not static or 0 <= p - back < pairs:
                    stages[back](p - back)

        def body(p, carry):
            step(p, False)
            return carry

        for p in range(last):
            step(p, True)
        lax.fori_loop(last, pairs, body, 0, unroll=UNROLL_BACK)
        for p in range(pairs, pairs + last):
            step(p, True)

    share = width // n_ray

    def red_copy(d, first):
        to = lax.rem(my_ray + d, n_ray)
        part = pl.ds(0, 1) if first else pl.ds(1, 2)
        sem = d + n_ray * first
        return pltpu.make_async_remote_copy(
            src_ref=acc.at[part, pl.ds(pl.multiple_of(to * share, share), share), :],
            dst_ref=red_ref.at[d, part],
            send_sem=red_send.at[sem],
            recv_sem=red_recv.at[sem],
            device_id={"ray": to},
            device_id_type=MESH,
        )

    pipelined(feature_grads, back_two, second_grads)
    for d in range(1, n_ray):
        red_copy(d, 0).start()
    pipelined(back_one, first_grads)
    for d in range(1, n_ray):
        red_copy(d, 1).start()

    def finish(p, carry):
        got = jnp.dot(p1_ref[p], w1b[...], preferred_element_type=F32).astype(BF16)
        o_ref[pl.ds(pl.multiple_of(p * span, span), span), :] = rows_of(got)
        out_copy(p).start()
        return carry

    lax.fori_loop(0, pairs, finish, 0, unroll=2)

    total = acc[:, pl.ds(pl.multiple_of(my_ray * share, share), share), :]
    for d in range(1, n_ray):
        red_copy(d, 0).wait()
        red_copy(d, 1).wait()
        total = total + red_ref[d]
    total = total * (1.0 / LOSS_SCALE)
    g1_ref[0] = total[0]
    g2_ref[0] = total[1]
    g3_ref[0] = total[2][:, :feat]
    g4_ref[...] = total[2].T[feat : feat + 1, :]

    @pl.loop(0, pairs)
    def _(p):
        out_copy(p).wait()


def hand_out(big_in, *refs):
    small_in, big_out, small_out, held, in_sem, out_sem, sems = (
        refs[:4],
        refs[4],
        refs[5:9],
        refs[9],
        refs[10],
        refs[11],
        refs[12],
    )
    size = held.shape[0] // PIECES
    pieces = [pl.ds(i * size, size) for i in range(PIECES)]
    arrive = [pltpu.make_async_copy(big_in.at[at], held.at[at], in_sem.at[i]) for i, at in enumerate(pieces)]
    leave = [pltpu.make_async_copy(held.at[at], big_out.at[at], out_sem.at[i]) for i, at in enumerate(pieces)]
    small = [pltpu.make_async_copy(small_in[i], small_out[i], sems.at[i]) for i in range(4)]
    for copy in arrive:
        copy.start()
    for copy in small:
        copy.start()
    for i in range(PIECES):
        arrive[i].wait()
        leave[i].start()
    for copy in leave + small:
        copy.wait()


def solution(mesh):
    n_brick, n_ray = mesh.shape["brick"], mesh.shape["ray"]

    def shards(samples_in, sample_count, step_length, view_flip, pixel_grad, w1, w2, wf, wd):
        rays, _, per_ray, width = samples_in.shape
        feat = pixel_grad.shape[0]
        rows = rays * per_ray
        pairs = rows // (2 * LANES)
        tiles = rows // LANES
        share = width // n_ray
        vmem = pl.BlockSpec(memory_space=pltpu.VMEM)
        hbm = pl.BlockSpec(memory_space=pl.ANY)
        pair_shape = (pairs, LANES, 2 * width)
        outs = pl.pallas_call(
            functools.partial(kernel, n_brick, n_ray, per_ray),
            out_shape=(
                jax.ShapeDtypeStruct((rows, width), BF16),
                jax.ShapeDtypeStruct((1, share, width), F32),
                jax.ShapeDtypeStruct((1, share, width), F32),
                jax.ShapeDtypeStruct((1, share, feat), F32),
                jax.ShapeDtypeStruct((1, share), F32),
            ),
            in_specs=[hbm] + [vmem] * 8,
            out_specs=(hbm,) + (vmem,) * 4,
            scratch_shapes=[
                pltpu.VMEM((rows, width), BF16),
                pltpu.VMEM((rows, width), BF16),
                pltpu.VMEM(pair_shape, BF16),
                pltpu.VMEM(pair_shape, BF16),
                pltpu.VMEM((pairs, 2 * width, LANES), BF16),
                pltpu.VMEM((pairs, 2 * width, LANES), BF16),
                pltpu.VMEM((pairs, 2 * width, LANES), BF16),
                pltpu.VMEM(pair_shape[1:], F32),
                pltpu.VMEM(pair_shape[1:], F32),
                pltpu.VMEM(pair_shape[1:], F32),
                pltpu.VMEM(pair_shape[1:], F32),
                pltpu.VMEM(pair_shape, F32),
                pltpu.VMEM(pair_shape, F32),
                pltpu.VMEM(pair_shape, BF16),
                pltpu.VMEM(pair_shape, BF16),
                pltpu.VMEM(pair_shape, BF16),
                pltpu.VMEM((rays, width), F32),
                pltpu.VMEM((rays, width), F32),
                pltpu.VMEM((tiles, LANES), F32),
                pltpu.VMEM((tiles, LANES), F32),
                pltpu.VMEM((tiles, LANES), F32),
                pltpu.VMEM((2 * width, 2 * width), BF16),
                pltpu.VMEM((2 * width, 2 * width), BF16),
                pltpu.VMEM((2 * width, 2 * width), BF16),
                pltpu.VMEM((2 * width, 2 * width), BF16),
                pltpu.VMEM((2 * width, 2 * width), BF16),
                pltpu.VMEM((3, width, width), F32),
                pltpu.VMEM((n_brick, 8, rays), F32),
                pltpu.VMEM((n_ray, 3, share, width), F32),
                pltpu.SemaphoreType.DMA,
                pltpu.SemaphoreType.DMA((pairs,)),
                pltpu.SemaphoreType.DMA((n_brick,)),
                pltpu.SemaphoreType.DMA((n_brick,)),
                pltpu.SemaphoreType.DMA((2 * n_ray,)),
                pltpu.SemaphoreType.DMA((2 * n_ray,)),
            ],
            compiler_params=pltpu.CompilerParams(
                collective_id=0, has_side_effects=True
            ),
        )(
            samples_in.reshape(rows, width),
            sample_count.reshape(1, rays),
            step_length.reshape(1, rays),
            view_flip.reshape(1, rays),
            pixel_grad,
            w1,
            w2,
            jnp.swapaxes(wf, 1, 2),
            wd,
        )
        outs = pl.pallas_call(
            hand_out,
            out_shape=tuple(jax.ShapeDtypeStruct(o.shape, o.dtype) for o in outs),
            in_specs=[hbm] + [vmem] * 4,
            out_specs=(hbm,) * 5,
            scratch_shapes=[
                pltpu.VMEM((rows, width), BF16),
                pltpu.SemaphoreType.DMA((PIECES,)),
                pltpu.SemaphoreType.DMA((PIECES,)),
                pltpu.SemaphoreType.DMA((4,)),
            ],
        )(*outs)
        return (outs[0].reshape(samples_in.shape),) + tuple(outs[1:])

    placed = (
        P(("groups", "ray"), "brick", None, None),
        P(("groups", "ray"), "brick"),
        P(("groups", "ray")),
        P(("groups", "ray")),
        P(None, ("groups", "ray")),
        P("brick", None, None),
        P("brick", None, None),
        P("brick", None, None),
        P("brick", None),
    )
    return jax.shard_map(
        shards,
        mesh=mesh,
        in_specs=placed,
        out_specs=(
            P(("groups", "ray"), "brick", None, None),
            P(("groups", "brick"), "ray", None),
            P(("groups", "brick"), "ray", None),
            P(("groups", "brick"), "ray", None),
            P(("groups", "brick"), "ray"),
        ),
        check_vma=False,
    )
```

profile of v0, /device:TPU:0, one launch (start us, length us, event | category | flops | bytes accessed | tf_op | source)
XLA Modules:
  0.0 30.2 jit_solution(6698739744085624437)
XLA Ops:
  0.6 26.4 %shard_map.128 = (bf16[8192,128]{1,0:T(8,128)(2,1)}, f32[1,32,128]{2,1,0:T(8,128)}, f32[1,32,128]{2,1,0:T(8,128)}, f32[1,32,64]{2,1,0:T(8,128)}, f32[1,32]{1,0:T(1,128)}) custom-call(bf16[8192,128]{1,0:T(8,128)(2,1)} %bitcast.8, s32[1,256]{1,0:T(1,128)} %bitcast.10, f32[1,256]{1,0:T(1,128)} %bitcast.11, s32[1,256]{1,0:T(1,128)} %bitcast.12, ...), custom_call_target="tpu_custom_call" | custom-call | tf_op jit(solution)/shard_map/pallas_call | solution.py:449
  27.0 3.2 %shard_map.129 = (bf16[8192,128]{1,0:T(8,128)(2,1)}, f32[1,32,128]{2,1,0:T(8,128)}, f32[1,32,128]{2,1,0:T(8,128)}, f32[1,32,64]{2,1,0:T(8,128)}, f32[1,32]{1,0:T(1,128)}) custom-call(bf16[8192,128]{1,0:T(8,128)(2,1)} %get-tuple-element.15.big_in, f32[1,32,128]{2,1,0:T(8,128)} %get-tuple-element.16.refs_0_, f32[1,32,128]{2,1,0:T(8,128)} %get-tuple-element.17.refs_1_, ...), custom_call_target="tpu_custom_call" | custom-call | tf_op jit(solution)/shard_map/pallas_call | solution.py:511
where the time goes:
time: 30.5 us; the launch traced here: 30.2 us
  Pallas kernels  29.6 us (97%)
  between operations  0.64 us (2%)
    pallas_call x1, Pallas kernels, shards(): pl.pallas_call(functools.partial(kernel, n_brick, n_ray, per_ray), out_sh...  26.4 us
    pallas_call x1, Pallas kernels, shards(): pl.pallas_call(hand_out, out_shape=tuple((jax.ShapeDtypeStruct(o.shape, o...  3.21 us

commit v1 on v0

--- a/solution.py
+++ b/solution.py
@@ -10,7 +10,7 @@
 LOSS_SCALE = 1024.0
 LANES = 256
 UNROLL_FORWARD = 1
-UNROLL_BACK = 1
+UNROLL_BACK = True
 PIECES = 8
 F32 = jnp.float32
 BF16 = jnp.bfloat16
@@ -216,7 +216,7 @@
     x_copy.wait()
     for p in range(4):
         forward_step(p, p % 2, True)
-    lax.fori_loop(2, pairs // 2, forward, 0)
+    lax.fori_loop(2, pairs // 2, forward, 0, unroll=True)
     for p in range(pairs, pairs + 4):
         forward_step(p, p % 2, True)
 
@@ -389,7 +389,7 @@
         out_copy(p).start()
         return carry
 
-    lax.fori_loop(0, pairs, finish, 0, unroll=2)
+    lax.fori_loop(0, pairs, finish, 0, unroll=True)
 
     total = acc[:, pl.ds(pl.multiple_of(my_ray * share, share), share), :]
     for d in range(1, n_ray):

time: 30.5 us -> 26.9 us (0.88)
  Pallas kernels: 29.6 us -> 26 us
    pallas_call x1, Pallas kernels: 26.4 us -> 22.8 us  [shards(): pl.pallas_call(functools.partial(kernel, n_brick, n_ray, per_ray), out_sh...]
where the time goes in v1:
time: 26.9 us; the launch traced here: 26.6 us
  Pallas kernels  26 us (97%)
  between operations  0.64 us (2%)
    pallas_call x1, Pallas kernels, shards(): pl.pallas_call(functools.partial(kernel, n_brick, n_ray, per_ray), out_sh...  22.8 us
    pallas_call x1, Pallas kernels, shards(): pl.pallas_call(hand_out, out_shape=tuple((jax.ShapeDtypeStruct(o.shape, o...  3.21 us

profile of v1, /device:TPU:0, one launch (start us, length us, event | category | flops | bytes accessed | tf_op | source)
XLA Modules:
  0.0 26.6 jit_solution(6033093159407663432)
XLA Ops:
  0.6 22.8 %shard_map.128 = (bf16[8192,128]{1,0:T(8,128)(2,1)}, f32[1,32,128]{2,1,0:T(8,128)}, f32[1,32,128]{2,1,0:T(8,128)}, f32[1,32,64]{2,1,0:T(8,128)}, f32[1,32]{1,0:T(1,128)}) custom-call(bf16[8192,128]{1,0:T(8,128)(2,1)} %bitcast.8, s32[1,256]{1,0:T(1,128)} %bitcast.10, f32[1,256]{1,0:T(1,128)} %bitcast.11, s32[1,256]{1,0:T(1,128)} %bitcast.12, ...), custom_call_target="tpu_custom_call" | custom-call | tf_op jit(solution)/shard_map/pallas_call | solution.py:449
  23.4 3.2 %shard_map.129 = (bf16[8192,128]{1,0:T(8,128)(2,1)}, f32[1,32,128]{2,1,0:T(8,128)}, f32[1,32,128]{2,1,0:T(8,128)}, f32[1,32,64]{2,1,0:T(8,128)}, f32[1,32]{1,0:T(1,128)}) custom-call(bf16[8192,128]{1,0:T(8,128)(2,1)} %get-tuple-element.15.big_in, f32[1,32,128]{2,1,0:T(8,128)} %get-tuple-element.16.refs_0_, f32[1,32,128]{2,1,0:T(8,128)} %get-tuple-element.17.refs_1_, ...), custom_call_target="tpu_custom_call" | custom-call | tf_op jit(solution)/shard_map/pallas_call | solution.py:511

commit v2 on v1

v2 whole, which is shorter than its diff:
```python
import functools

import jax
import jax.numpy as jnp
from jax import lax
from jax.experimental import pallas as pl
from jax.experimental.pallas import tpu as pltpu
from jax.sharding import PartitionSpec as P

LOSS_SCALE = 1024.0
LANES = 256
CHUNKS = 1
X_PIECES = 4
K_TILES = 8
F32 = jnp.float32
BF16 = jnp.bfloat16
MESH = pl.DeviceIdType.MESH


def iota(shape, dim):
    return lax.broadcasted_iota(jnp.int32, shape, dim)


def split_two(v):
    hi = v.astype(BF16).astype(F32)
    return hi, v - hi


def split_three(v):
    hi, rest = split_two(v)
    mid, low = split_two(rest)
    return hi, mid, low


def dot_exact(v, m):
    rows = v.shape[0]
    out = jnp.dot(
        jnp.concatenate(split_three(v), axis=0).astype(BF16), m, preferred_element_type=F32
    )
    return out[:rows] + out[rows : 2 * rows] + out[2 * rows :]


def contract_rows(left, right):
    return lax.dot_general(left, right, (((0,), (0,)), ((), ())), preferred_element_type=F32)


def block_diag(w):
    z = jnp.zeros_like(w)
    return jnp.concatenate(
        [jnp.concatenate([w, z], axis=1), jnp.concatenate([z, w], axis=1)], axis=0
    )


def side(v, right):
    z = jnp.zeros_like(v)
    return jnp.concatenate([z, v] if right else [v, z], axis=1)


def silu_pair(half):
    t = jnp.tanh(half)
    a = 1.0 + t
    h = half * a
    slope = a + h * (1.0 - t)
    return h, slope


def kernel(
    n_brick,
    n_ray,
    per_ray,
    x_hbm,
    count_hbm,
    step_hbm,
    flip_hbm,
    pg_hbm,
    w1_hbm,
    w2_hbm,
    wf_hbm,
    wd_hbm,
    o_ref,
    g1_ref,
    g2_ref,
    g3_ref,
    g4_ref,
    x_ref,
    count_ref,
    step_ref,
    flip_ref,
    pg_ref,
    w1_ref,
    w2_ref,
    wf_ref,
    wd_ref,
    xt_ref,
    h1_ref,
    h1t_ref,
    h2_ref,
    p1_ref,
    p2_ref,
    s1_ref,
    s2_ref,
    v_ref,
    sc_ref,
    q_ref,
    lg_ref,
    len_ref,
    c_ref,
    u_ref,
    w1f,
    w2f,
    w1b,
    w2b,
    wfb,
    acc,
    ex_ref,
    red_ref,
    in_sem,
    x_sem,
    ex_send,
    ex_recv,
    red_send,
    red_recv,
):
    rows, width = x_ref.shape
    feat, rays = pg_ref.shape
    group = LANES // per_ray
    tiles = rows // LANES
    pairs = tiles // 2
    span = 2 * LANES
    half = LANES // 2

    small = [
        pltpu.make_async_copy(src, dst, in_sem.at[i])
        for i, (src, dst) in enumerate(
            (
                (w1_hbm, w1_ref),
                (w2_hbm, w2_ref),
                (wf_hbm, wf_ref),
                (wd_hbm, wd_ref),
                (pg_hbm, pg_ref),
                (count_hbm, count_ref),
                (step_hbm, step_ref),
                (flip_hbm, flip_ref),
            )
        )
    ]
    piece = rows // X_PIECES
    pieces = [
        pltpu.make_async_copy(
            x_hbm.at[pl.ds(i * piece, piece)], x_ref.at[pl.ds(i * piece, piece)], x_sem.at[i]
        )
        for i in range(X_PIECES)
    ]
    small[0].start()
    pieces[0].start()
    for copy in small[1:] + pieces[1:]:
        copy.start()

    my_brick = lax.axis_index("brick")
    my_ray = lax.axis_index("ray")
    barrier = pltpu.get_barrier_semaphore()
    for d in range(1, n_brick):
        pl.semaphore_signal(
            barrier, inc=1, device_id={"brick": lax.rem(my_brick + d, n_brick)}, device_id_type=MESH
        )
    for d in range(1, n_ray):
        pl.semaphore_signal(
            barrier, inc=1, device_id={"ray": lax.rem(my_ray + d, n_ray)}, device_id_type=MESH
        )

    group_mask = (iota((group, LANES), 0) == iota((group, LANES), 1) // per_ray).astype(F32)
    unit = (iota((8, width), 1) == feat).astype(F32)
    rays_c = rays // CHUNKS
    tiles_c = tiles // CHUNKS
    pairs_c = pairs // CHUNKS
    spread = (iota((rays_c, LANES), 0) % group == iota((rays_c, LANES), 1) // per_ray).astype(BF16)
    gather = (iota((LANES, rays_c), 1) % group == iota((LANES, rays_c), 0) // per_ray).astype(BF16)
    owner = (iota((tiles_c, rays_c), 1) // group == iota((tiles_c, rays_c), 0)).astype(F32)
    from_s, to_s = iota((LANES, LANES), 0), iota((LANES, LANES), 1)
    same = from_s // per_ray == to_s // per_ray
    upto = (same & (from_s <= to_s)).astype(BF16)
    later = (same & (from_s > to_s)).astype(BF16)

    def to_samples(*ray_rows):
        out = dot_exact(jnp.concatenate([owner * r for r in ray_rows], axis=0), spread)
        return [out[i * tiles_c : (i + 1) * tiles_c] for i in range(len(ray_rows))]

    def to_rays(*sample_values):
        out = dot_exact(jnp.concatenate(sample_values, axis=0), gather)
        return [
            jnp.sum(out[i * tiles_c : (i + 1) * tiles_c] * owner, axis=0, keepdims=True)
            for i in range(len(sample_values))
        ]

    small[0].wait()
    w1 = w1_ref[0].astype(F32)
    w1f[...] = block_diag(w1 * 0.5).astype(BF16)

    def pair_of(ref, p):
        return jnp.concatenate([ref[2 * p], ref[2 * p + 1]], axis=1)

    def put_pair(ref, p, v):
        ref[2 * p] = v[:, :width]
        ref[2 * p + 1] = v[:, width:]

    def put_turned(ref, p, v):
        for k in range(2):
            t = v[:, k * width : (k + 1) * width].T
            for j in range(2):
                ref[2 * p + k, j] = t[:, j * half : (j + 1) * half]

    def first_layer(p):
        if p % (pairs // X_PIECES) == 0:
            pieces[p // (pairs // X_PIECES)].wait()
        x = jnp.concatenate(
            [x_ref[pl.ds(p * span, LANES), :], x_ref[pl.ds(p * span + LANES, LANES), :]], axis=1
        )
        h1, s1 = silu_pair(jnp.dot(x, w1f[...], preferred_element_type=F32))
        h1 = h1.astype(BF16)
        put_pair(h1_ref, p, h1)
        s1_ref[p] = s1
        put_turned(h1t_ref, p, h1)
        put_turned(xt_ref, p, x)

    def second_layer(p):
        h2, s2 = silu_pair(jnp.dot(pair_of(h1_ref, p), w2f[...], preferred_element_type=F32))
        put_pair(h2_ref, p, h2.astype(BF16))
        s2_ref[p] = s2

    def heads(p):
        left = []
        for k in range(2):
            hi, low = split_two(v_ref[pl.ds((2 * p + k) * group, group), :])
            left += [side(hi, k), side(low, k), side(wd_rows, k)]
        left = jnp.concatenate(left, axis=0).astype(BF16)
        got = lax.dot_general(
            left, pair_of(h2_ref, p), (((1,), (1,)), ((), ())), preferred_element_type=F32
        )
        for k in range(2):
            base = k * (2 * group + 8)
            dots = got[base : base + group] + got[base + group : base + 2 * group]
            q_ref[pl.ds(2 * p + k, 1), :] = jnp.sum(dots * group_mask, axis=0, keepdims=True)
            lg_ref[pl.ds(2 * p + k, 1), :] = got[base + 2 * group : base + 2 * group + 1]

    first_layer(0)
    for copy in small[1:]:
        copy.wait()
    w2 = w2_ref[0].astype(F32)
    wd = wd_ref[...].astype(F32)
    w2f[...] = block_diag(w2 * 0.5).astype(BF16)
    wide = jnp.concatenate(
        [wf_ref[0].astype(F32), wd, jnp.zeros((width - feat - 1, width), F32)], axis=0
    )
    wfb[...] = block_diag(wide * 0.5).astype(BF16)
    w1b[...] = block_diag(w1.T).astype(BF16)
    w2b[...] = block_diag(w2.T * 0.5).astype(BF16)
    scaled = jnp.concatenate(
        [LOSS_SCALE * pg_ref[...], jnp.zeros((width - feat, rays), F32)], axis=0
    ).T
    sc_ref[...] = scaled
    v_ref[...] = dot_exact(scaled, wide.astype(BF16))
    wd_rows = jnp.broadcast_to(wd, (8, width))
    for ch in range(CHUNKS):
        at = slice(ch * rays_c, (ch + 1) * rays_c)
        count, length = to_samples(count_ref[:, at].astype(F32), step_ref[:, at])
        len_ref[pl.ds(ch * tiles_c, tiles_c), :] = jnp.where(
            (iota((tiles_c, LANES), 1) % per_ray).astype(F32) < count, length, 0.0
        )

    def middle(ch):
        mine = pl.ds(ch * tiles_c, tiles_c)
        logits = lg_ref[mine, :]
        q = q_ref[mine, :]
        length = len_ref[mine, :]
        softplus = jnp.maximum(logits, 0.0) + jnp.log1p(jnp.exp(-jnp.abs(logits)))
        depth_step = softplus * length
        depth_incl = dot_exact(depth_step, upto)
        half_step = jnp.tanh(0.5 * depth_step)
        weights = jnp.exp(depth_step - depth_incl) * (2.0 * half_step / (1.0 + half_step))
        weighted = weights * q
        brick_depth, brick_dot = to_rays(depth_step, weighted)
        ex_ref[ch, 0] = jnp.concatenate([brick_depth, brick_dot, jnp.zeros((6, rays_c), F32)], axis=0)
        c_ref[mine, :] = weights
        q_ref[mine, :] = jnp.exp(-depth_incl) * q - dot_exact(weighted, later)
        len_ref[mine, :] = length * (0.5 + 0.5 * jnp.tanh(0.5 * logits))

    def ex_copy(ch, d):
        return pltpu.make_async_remote_copy(
            src_ref=ex_ref.at[ch, 0],
            dst_ref=ex_ref.at[ch, d],
            send_sem=ex_send.at[ch, d],
            recv_sem=ex_recv.at[ch, d],
            device_id={"brick": lax.rem(my_brick + d, n_brick)},
            device_id_type=MESH,
        )

    def send(ch):
        if ch == 0:
            pl.semaphore_wait(barrier, n_brick + n_ray - 2)
        for d in range(1, n_brick):
            ex_copy(ch, d).start()

    def composite(ch):
        for d in range(1, n_brick):
            ex_copy(ch, d).wait()
        mine = pl.ds(ch * tiles_c, tiles_c)
        there = [ex_ref[ch, lax.rem(my_brick - k + n_brick, n_brick)] for k in range(n_brick)]

        def walk(order, is_past):
            gap = jnp.zeros((1, rays_c), F32)
            seen = jnp.zeros((1, rays_c), F32)
            for k in order:
                past = jnp.where(is_past(k), 1.0, 0.0)
                seen = seen + past * jnp.exp(-gap) * there[k][1:2]
                gap = gap + past * there[k][0:1]
            return gap, seen

        upper_depth, upper_seen = walk(range(n_brick), lambda k: k > my_brick)
        lower_depth, lower_seen = walk(range(n_brick - 1, -1, -1), lambda k: k < my_brick)
        flipped = flip_ref[:, ch * rays_c : (ch + 1) * rays_c] > 0
        through_front = jnp.exp(-jnp.where(flipped, upper_depth, lower_depth))
        behind = jnp.where(flipped, lower_seen, upper_seen)
        brick_depth = ex_ref[ch, 0, 0:1]
        front, brick_grad = to_samples(
            through_front, -through_front * jnp.exp(-brick_depth) * behind
        )
        lg_ref[mine, :] = (front * q_ref[mine, :] + brick_grad) * len_ref[mine, :]
        c_ref[mine, :] = front * c_ref[mine, :]

    def feature_grads(p):
        left, right = [], []
        sums = []
        for k in range(2):
            t = 2 * p + k
            c_hi, c_low = split_two(c_ref[pl.ds(t, 1), :] * group_mask)
            lgm = lg_ref[pl.ds(t, 1), :] * group_mask
            s_hi, s_low = split_two(sc_ref[pl.ds(t * group, group), :])
            left += [c_hi, c_hi, c_low, lgm]
            sums += [c_hi, c_low, lgm]
            right += [side(s_hi, k), side(s_low, k), side(s_hi, k), side(unit, k)]
        left = jnp.concatenate(left, axis=0).astype(BF16)
        right = jnp.concatenate(right, axis=0).astype(BF16)
        sums = jnp.concatenate(sums, axis=0).astype(BF16)
        fg = contract_rows(left, right).astype(BF16)
        h2g = jnp.dot(fg, wfb[...], preferred_element_type=F32)
        put_pair(p2_ref, p, (h2g * s2_ref[p]).astype(BF16))
        got = jnp.dot(sums, pair_of(h2_ref, p), preferred_element_type=F32)
        dens = jnp.zeros((group, width), F32)
        for k in range(2):
            base = 3 * group * k
            mine = got[:, k * width : (k + 1) * width]
            u_ref[pl.ds((2 * p + k) * group, group), :] = (
                mine[base : base + group] + mine[base + group : base + 2 * group]
            )
            dens = dens + mine[base + 2 * group : base + 3 * group]
        return dens

    def back_one(p):
        h1g = jnp.dot(pair_of(p2_ref, p), w2b[...], preferred_element_type=F32)
        put_pair(p1_ref, p, (h1g * s1_ref[p]).astype(BF16))

    def finish(p):
        got = jnp.dot(pair_of(p1_ref, p), w1b[...], preferred_element_type=F32).astype(BF16)
        o_ref[pl.ds(p * span, LANES), :] = got[:, :width]
        o_ref[pl.ds(p * span + LANES, LANES), :] = got[:, width:]

    def weight_grad(turned, grads):
        total = None
        for t0 in range(0, tiles, K_TILES):
            left = jnp.concatenate(
                [turned[t, j] for t in range(t0, t0 + K_TILES) for j in range(2)], axis=1
            )
            right = grads[pl.ds(t0, K_TILES)].reshape(K_TILES * LANES, width)
            got = jnp.dot(left, right, preferred_element_type=F32)
            total = got if total is None else total + got
        return total

    share = width // n_ray

    def red_copy(d, first):
        to = lax.rem(my_ray + d, n_ray)
        part = pl.ds(0, 1) if first else pl.ds(1, 2)
        sem = d + n_ray * first
        return pltpu.make_async_remote_copy(
            src_ref=acc.at[part, pl.ds(pl.multiple_of(to * share, share), share), :],
            dst_ref=red_ref.at[d, part],
            send_sem=red_send.at[sem],
            recv_sem=red_recv.at[sem],
            device_id={"ray": to},
            device_id_type=MESH,
        )

    for p in range(1, pairs + 2):
        if p < pairs:
            first_layer(p)
        if p - 1 < pairs:
            second_layer(p - 1)
        if p - 2 >= 0:
            heads(p - 2)
        for ch in range(CHUNKS):
            if p - 2 == (ch + 1) * pairs_c - 1:
                middle(ch)
                send(ch)

    dens = jnp.zeros((group, width), F32)
    for p in range(pairs + 1):
        if p % pairs_c == 0 and p < pairs:
            composite(p // pairs_c)
        if p < pairs:
            dens = dens + feature_grads(p)
        if p >= 1:
            back_one(p - 1)
    acc[1] = weight_grad(h1t_ref, p2_ref)
    u_hi, u_low = split_two(u_ref[...])
    s_hi, s_low = split_two(sc_ref[...])
    parts = split_three(dens)
    acc[2] = contract_rows(
        jnp.concatenate([u_hi, u_hi, u_low, *parts], axis=0).astype(BF16),
        jnp.concatenate([s_hi, s_low, s_hi, unit, unit, unit], axis=0).astype(BF16),
    )
    for d in range(1, n_ray):
        red_copy(d, 0).start()
    acc[0] = weight_grad(xt_ref, p1_ref)
    for d in range(1, n_ray):
        red_copy(d, 1).start()
    for p in range(pairs):
        finish(p)

    total = acc[:, pl.ds(pl.multiple_of(my_ray * share, share), share), :]
    for d in range(1, n_ray):
        red_copy(d, 0).wait()
        red_copy(d, 1).wait()
        total = total + red_ref[d]
    total = total * (1.0 / LOSS_SCALE)
    g1_ref[0] = total[0]
    g2_ref[0] = total[1]
    g3_ref[0] = total[2][:, :feat]
    g4_ref[...] = total[2].T[feat : feat + 1, :]


def hand_out(*refs):
    held, out, sems = refs[:5], refs[5:10], refs[10]
    copies = [pltpu.make_async_copy(held[i], out[i], sems.at[i]) for i in range(5)]
    for copy in copies:
        copy.start()
    for copy in copies:
        copy.wait()


def solution(mesh):
    n_brick, n_ray = mesh.shape["brick"], mesh.shape["ray"]

    def shards(samples_in, sample_count, step_length, view_flip, pixel_grad, w1, w2, wf, wd):
        rays, _, per_ray, width = samples_in.shape
        feat = pixel_grad.shape[0]
        rows = rays * per_ray
        pairs = rows // (2 * LANES)
        tiles = rows // LANES
        share = width // n_ray
        vmem = pl.BlockSpec(memory_space=pltpu.VMEM)
        hbm = pl.BlockSpec(memory_space=pl.ANY)
        tile_shape = (tiles, LANES, width)
        turned_shape = (tiles, 2, width, LANES // 2)
        outs = pl.pallas_call(
            functools.partial(kernel, n_brick, n_ray, per_ray),
            out_shape=(
                pltpu.VMEM((rows, width), BF16),
                pltpu.VMEM((1, share, width), F32),
                pltpu.VMEM((1, share, width), F32),
                pltpu.VMEM((1, share, feat), F32),
                pltpu.VMEM((1, share), F32),
            ),
            in_specs=[hbm] * 9,
            out_specs=(vmem,) * 5,
            scratch_shapes=[
                pltpu.VMEM((rows, width), BF16),
                pltpu.VMEM((1, rays), jnp.int32),
                pltpu.VMEM((1, rays), F32),
                pltpu.VMEM((1, rays), jnp.int32),
                pltpu.VMEM((feat, rays), F32),
                pltpu.VMEM((1, width, width), BF16),
                pltpu.VMEM((1, width, width), BF16),
                pltpu.VMEM((1, feat, width), BF16),
                pltpu.VMEM((1, width), BF16),
                pltpu.VMEM(turned_shape, BF16),
                pltpu.VMEM(tile_shape, BF16),
                pltpu.VMEM(turned_shape, BF16),
                pltpu.VMEM(tile_shape, BF16),
                pltpu.VMEM(tile_shape, BF16),
                pltpu.VMEM(tile_shape, BF16),
                pltpu.VMEM((pairs, LANES, 2 * width), F32),
                pltpu.VMEM((pairs, LANES, 2 * width), F32),
                pltpu.VMEM((rays, width), F32),
                pltpu.VMEM((rays, width), F32),
                pltpu.VMEM((tiles, LANES), F32),
                pltpu.VMEM((tiles, LANES), F32),
                pltpu.VMEM((tiles, LANES), F32),
                pltpu.VMEM((tiles, LANES), F32),
                pltpu.VMEM((rays, width), F32),
                pltpu.VMEM((2 * width, 2 * width), BF16),
                pltpu.VMEM((2 * width, 2 * width), BF16),
                pltpu.VMEM((2 * width, 2 * width), BF16),
                pltpu.VMEM((2 * width, 2 * width), BF16),
                pltpu.VMEM((2 * width, 2 * width), BF16),
                pltpu.VMEM((3, width, width), F32),
                pltpu.VMEM((CHUNKS, n_brick, 8, rays // CHUNKS), F32),
                pltpu.VMEM((n_ray, 3, share, width), F32),
                pltpu.SemaphoreType.DMA((8,)),
                pltpu.SemaphoreType.DMA((X_PIECES,)),
                pltpu.SemaphoreType.DMA((CHUNKS, n_brick)),
                pltpu.SemaphoreType.DMA((CHUNKS, n_brick)),
                pltpu.SemaphoreType.DMA((2 * n_ray,)),
                pltpu.SemaphoreType.DMA((2 * n_ray,)),
            ],
            compiler_params=pltpu.CompilerParams(
                collective_id=0, has_side_effects=True, vmem_limit_bytes=52 * 1024 * 1024
            ),
        )(
            samples_in.reshape(rows, width),
            sample_count.reshape(1, rays),
            step_length.reshape(1, rays),
            view_flip.reshape(1, rays),
            pixel_grad,
            w1,
            w2,
            jnp.swapaxes(wf, 1, 2),
            wd,
        )
        outs = pl.pallas_call(
            hand_out,
            out_shape=tuple(jax.ShapeDtypeStruct(o.shape, o.dtype) for o in outs),
            in_specs=[vmem] * 5,
            out_specs=(hbm,) * 5,
            scratch_shapes=[pltpu.SemaphoreType.DMA((5,))],
            compiler_params=pltpu.CompilerParams(vmem_limit_bytes=4 * 1024 * 1024),
        )(*[pltpu.with_memory_space_constraint(o, pltpu.VMEM) for o in outs])
        return (outs[0].reshape(samples_in.shape),) + tuple(outs[1:])

    placed = (
        P(("groups", "ray"), "brick", None, None),
        P(("groups", "ray"), "brick"),
        P(("groups", "ray")),
        P(("groups", "ray")),
        P(None, ("groups", "ray")),
        P("brick", None, None),
        P("brick", None, None),
        P("brick", None, None),
        P("brick", None),
    )
    return jax.shard_map(
        shards,
        mesh=mesh,
        in_specs=placed,
        out_specs=(
            P(("groups", "ray"), "brick", None, None),
            P(("groups", "brick"), "ray", None),
            P(("groups", "brick"), "ray", None),
            P(("groups", "brick"), "ray", None),
            P(("groups", "brick"), "ray"),
        ),
        check_vma=False,
    )
```

time: 26.9 us -> 22.9 us (0.85)
  Pallas kernels: 26 us -> 22.1 us
    pallas_call x1, Pallas kernels: 22.8 us -> 20.7 us  [shards(): pl.pallas_call(functools.partial(kernel, n_brick, n_ray, per_ray), out_sh...]
    pallas_call x1, Pallas kernels: 3.21 us -> 1.37 us  [shards(): pl.pallas_call(hand_out, out_shape=tuple((jax.ShapeDtypeStruct(o.shape, o...]
where the time goes in v2:
time: 22.9 us; the launch traced here: 22.7 us
  Pallas kernels  22.1 us (97%)
  between operations  0.64 us (3%)
    pallas_call x1, Pallas kernels, shards(): pl.pallas_call(functools.partial(kernel, n_brick, n_ray, per_ray), out_sh...  20.7 us
    pallas_call x1, Pallas kernels, shards(): pl.pallas_call(hand_out, out_shape=tuple((jax.ShapeDtypeStruct(o.shape, o...  1.37 us

profile of v2, /device:TPU:0, one launch (start us, length us, event | category | flops | bytes accessed | tf_op | source)
XLA Modules:
  0.0 22.7 jit_solution(330744033818979458)
XLA Ops:
  0.6 20.7 %shard_map.128 = (bf16[8192,128]{1,0:T(8,128)(2,1)S(1)}, f32[1,32,128]{2,1,0:T(8,128)S(1)}, f32[1,32,128]{2,1,0:T(8,128)S(1)}, f32[1,32,64]{2,1,0:T(8,128)S(1)}, f32[1,32]{1,0:T(1,128)S(1)}) custom-call(bf16[8192,128]{1,0:T(8,128)(2,1)} %bitcast.8, s32[1,256]{1,0:T(1,128)} %bitcast.10, f32[1,256]{1,0:T(1,128)} %bitcast.11, s32[1,256]{1,0:T(1,128)} %bitcast.12, ...), custom_call_target="tpu_custom_call" | custom-call | tf_op jit(solution)/shard_map/pallas_call | solution.py:464
  21.4 1.4 %shard_map.129 = (bf16[8192,128]{1,0:T(8,128)(2,1)}, f32[1,32,128]{2,1,0:T(8,128)}, f32[1,32,128]{2,1,0:T(8,128)}, f32[1,32,64]{2,1,0:T(8,128)}, f32[1,32]{1,0:T(1,128)}) custom-call(bf16[8192,128]{1,0:T(8,128)(2,1)S(1)} %get-tuple-element.15.refs_0_, f32[1,32,128]{2,1,0:T(8,128)S(1)} %get-tuple-element.16.refs_1_, ...), custom_call_target="tpu_custom_call" | custom-call | tf_op jit(solution)/shard_map/pallas_call | solution.py:529

commit v3 on v2

--- a/solution.py
+++ b/solution.py
@@ -9,9 +9,9 @@
 
 LOSS_SCALE = 1024.0
 LANES = 256
-CHUNKS = 1
-X_PIECES = 4
+CHUNKS = 2
 K_TILES = 8
+HEAD_START = 3
 F32 = jnp.float32
 BF16 = jnp.bfloat16
 MESH = pl.DeviceIdType.MESH
@@ -144,12 +144,12 @@
             )
         )
     ]
-    piece = rows // X_PIECES
+    piece = rows // CHUNKS
     pieces = [
         pltpu.make_async_copy(
             x_hbm.at[pl.ds(i * piece, piece)], x_ref.at[pl.ds(i * piece, piece)], x_sem.at[i]
         )
-        for i in range(X_PIECES)
+        for i in range(CHUNKS)
     ]
     small[0].start()
     pieces[0].start()
@@ -192,7 +192,8 @@
             for i in range(len(sample_values))
         ]
 
-    small[0].wait()
+    for copy in small:
+        copy.wait()
     w1 = w1_ref[0].astype(F32)
     w1f[...] = block_diag(w1 * 0.5).astype(BF16)
 
@@ -205,22 +206,21 @@
 
     def put_turned(ref, p, v):
         for k in range(2):
-            t = v[:, k * width : (k + 1) * width].T
-            for j in range(2):
-                ref[2 * p + k, j] = t[:, j * half : (j + 1) * half]
+            ref[2 * p + k] = v[:, k * width : (k + 1) * width].T
+
+    def x_pair(p):
+        return jnp.concatenate(
+            [x_ref[pl.ds(p * span, LANES), :], x_ref[pl.ds(p * span + LANES, LANES), :]], axis=1
+        )
 
     def first_layer(p):
-        if p % (pairs // X_PIECES) == 0:
-            pieces[p // (pairs // X_PIECES)].wait()
-        x = jnp.concatenate(
-            [x_ref[pl.ds(p * span, LANES), :], x_ref[pl.ds(p * span + LANES, LANES), :]], axis=1
-        )
-        h1, s1 = silu_pair(jnp.dot(x, w1f[...], preferred_element_type=F32))
-        h1 = h1.astype(BF16)
-        put_pair(h1_ref, p, h1)
+        h1, s1 = silu_pair(jnp.dot(x_pair(p), w1f[...], preferred_element_type=F32))
+        put_pair(h1_ref, p, h1.astype(BF16))
         s1_ref[p] = s1
-        put_turned(h1t_ref, p, h1)
-        put_turned(xt_ref, p, x)
+
+    def turn(p):
+        put_turned(h1t_ref, p, pair_of(h1_ref, p))
+        put_turned(xt_ref, p, x_pair(p))
 
     def second_layer(p):
         h2, s2 = silu_pair(jnp.dot(pair_of(h1_ref, p), w2f[...], preferred_element_type=F32))
@@ -242,9 +242,6 @@
             q_ref[pl.ds(2 * p + k, 1), :] = jnp.sum(dots * group_mask, axis=0, keepdims=True)
             lg_ref[pl.ds(2 * p + k, 1), :] = got[base + 2 * group : base + 2 * group + 1]
 
-    first_layer(0)
-    for copy in small[1:]:
-        copy.wait()
     w2 = w2_ref[0].astype(F32)
     wd = wd_ref[...].astype(F32)
     w2f[...] = block_diag(w2 * 0.5).astype(BF16)
@@ -329,21 +326,25 @@
 
     def feature_grads(p):
         left, right = [], []
-        sums = []
         for k in range(2):
             t = 2 * p + k
             c_hi, c_low = split_two(c_ref[pl.ds(t, 1), :] * group_mask)
             lgm = lg_ref[pl.ds(t, 1), :] * group_mask
             s_hi, s_low = split_two(sc_ref[pl.ds(t * group, group), :])
             left += [c_hi, c_hi, c_low, lgm]
-            sums += [c_hi, c_low, lgm]
             right += [side(s_hi, k), side(s_low, k), side(s_hi, k), side(unit, k)]
         left = jnp.concatenate(left, axis=0).astype(BF16)
         right = jnp.concatenate(right, axis=0).astype(BF16)
+        fg = contract_rows(left, right).astype(BF16)
+        put_pair(p1_ref, p, fg)
+
+    def ray_sums(p):
+        sums = []
+        for k in range(2):
+            t = 2 * p + k
+            c_hi, c_low = split_two(c_ref[pl.ds(t, 1), :] * group_mask)
+            sums += [c_hi, c_low, lg_ref[pl.ds(t, 1), :] * group_mask]
         sums = jnp.concatenate(sums, axis=0).astype(BF16)
-        fg = contract_rows(left, right).astype(BF16)
-        h2g = jnp.dot(fg, wfb[...], preferred_element_type=F32)
-        put_pair(p2_ref, p, (h2g * s2_ref[p]).astype(BF16))
         got = jnp.dot(sums, pair_of(h2_ref, p), preferred_element_type=F32)
         dens = jnp.zeros((group, width), F32)
         for k in range(2):
@@ -355,6 +356,10 @@
             dens = dens + mine[base + 2 * group : base + 3 * group]
         return dens
 
+    def back_two(p):
+        h2g = jnp.dot(pair_of(p1_ref, p), wfb[...], preferred_element_type=F32)
+        put_pair(p2_ref, p, (h2g * s2_ref[p]).astype(BF16))
+
     def back_one(p):
         h1g = jnp.dot(pair_of(p2_ref, p), w2b[...], preferred_element_type=F32)
         put_pair(p1_ref, p, (h1g * s1_ref[p]).astype(BF16))
@@ -368,7 +373,7 @@
         total = None
         for t0 in range(0, tiles, K_TILES):
             left = jnp.concatenate(
-                [turned[t, j] for t in range(t0, t0 + K_TILES) for j in range(2)], axis=1
+                [turned[t] for t in range(t0, t0 + K_TILES)], axis=1
             )
             right = grads[pl.ds(t0, K_TILES)].reshape(K_TILES * LANES, width)
             got = jnp.dot(left, right, preferred_element_type=F32)
@@ -390,26 +395,50 @@
             device_id_type=MESH,
         )
 
-    for p in range(1, pairs + 2):
-        if p < pairs:
+    def late_layers(ch):
+        first, last = ch * pairs_c, (ch + 1) * pairs_c
+        for p in range(first, last + 2, 2):
+            for k in (p, p + 1):
+                if k < last:
+                    second_layer(k)
+            for k in (p - 2, p - 1):
+                if k >= first:
+                    heads(k)
+
+    pieces[0].wait()
+    for p in range(pairs_c):
+        first_layer(p)
+    late_layers(0)
+    for ch in range(1, CHUNKS):
+        first = ch * pairs_c
+        pieces[ch].wait()
+        middle(ch - 1)
+        for p in range(first, first + HEAD_START):
             first_layer(p)
-        if p - 1 < pairs:
-            second_layer(p - 1)
-        if p - 2 >= 0:
-            heads(p - 2)
-        for ch in range(CHUNKS):
-            if p - 2 == (ch + 1) * pairs_c - 1:
-                middle(ch)
-                send(ch)
+        send(ch - 1)
+        for p in range(first + HEAD_START, first + pairs_c):
+            first_layer(p)
+        late_layers(ch)
+    middle(CHUNKS - 1)
+    send(CHUNKS - 1)
+    for p in range(pairs):
+        turn(p)
 
     dens = jnp.zeros((group, width), F32)
-    for p in range(pairs + 1):
-        if p % pairs_c == 0 and p < pairs:
-            composite(p // pairs_c)
-        if p < pairs:
-            dens = dens + feature_grads(p)
-        if p >= 1:
-            back_one(p - 1)
+    for ch in range(CHUNKS):
+        first, last = ch * pairs_c, (ch + 1) * pairs_c
+        composite(ch)
+        if ch > 0:
+            for p in range(first - pairs_c, first):
+                back_one(p)
+        for p in range(first, last):
+            feature_grads(p)
+        for p in range(first, last):
+            dens = dens + ray_sums(p)
+        for p in range(first, last):
+            back_two(p)
+    for p in range(pairs - pairs_c, pairs):
+        back_one(p)
     acc[1] = weight_grad(h1t_ref, p2_ref)
     u_hi, u_low = split_two(u_ref[...])
     s_hi, s_low = split_two(sc_ref[...])
@@ -460,7 +489,7 @@
         vmem = pl.BlockSpec(memory_space=pltpu.VMEM)
         hbm = pl.BlockSpec(memory_space=pl.ANY)
         tile_shape = (tiles, LANES, width)
-        turned_shape = (tiles, 2, width, LANES // 2)
+        turned_shape = (tiles, width, LANES)
         outs = pl.pallas_call(
             functools.partial(kernel, n_brick, n_ray, per_ray),
             out_shape=(
@@ -506,7 +535,7 @@
                 pltpu.VMEM((CHUNKS, n_brick, 8, rays // CHUNKS), F32),
                 pltpu.VMEM((n_ray, 3, share, width), F32),
                 pltpu.SemaphoreType.DMA((8,)),
-                pltpu.SemaphoreType.DMA((X_PIECES,)),
+                pltpu.SemaphoreType.DMA((CHUNKS,)),
                 pltpu.SemaphoreType.DMA((CHUNKS, n_brick)),
                 pltpu.SemaphoreType.DMA((CHUNKS, n_brick)),
                 pltpu.SemaphoreType.DMA((2 * n_ray,)),

time: 22.9 us -> 20.6 us (0.90)
  Pallas kernels: 22.1 us -> 19.8 us
    pallas_call x1, Pallas kernels: 20.7 us -> 18.4 us  [shards(): pl.pallas_call(functools.partial(kernel, n_brick, n_ray, per_ray), out_sh...]
where the time goes in v3:
time: 20.6 us; the launch traced here: 20.4 us
  Pallas kernels  19.8 us (96%)
  between operations  0.64 us (3%)
    pallas_call x1, Pallas kernels, shards(): pl.pallas_call(functools.partial(kernel, n_brick, n_ray, per_ray), out_sh...  18.4 us
    pallas_call x1, Pallas kernels, shards(): pl.pallas_call(hand_out, out_shape=tuple((jax.ShapeDtypeStruct(o.shape, o...  1.37 us

profile of v3, /device:TPU:0, one launch (start us, length us, event | category | flops | bytes accessed | tf_op | source)
XLA Modules:
  0.0 20.4 jit_solution(2573140287972659868)
XLA Ops:
  0.6 18.4 %shard_map.128 = (bf16[8192,128]{1,0:T(8,128)(2,1)S(1)}, f32[1,32,128]{2,1,0:T(8,128)S(1)}, f32[1,32,128]{2,1,0:T(8,128)S(1)}, f32[1,32,64]{2,1,0:T(8,128)S(1)}, f32[1,32]{1,0:T(1,128)S(1)}) custom-call(bf16[8192,128]{1,0:T(8,128)(2,1)} %bitcast.8, s32[1,256]{1,0:T(1,128)} %bitcast.10, f32[1,256]{1,0:T(1,128)} %bitcast.11, s32[1,256]{1,0:T(1,128)} %bitcast.12, ...), custom_call_target="tpu_custom_call" | custom-call | tf_op jit(solution)/shard_map/pallas_call | solution.py:493
  19.0 1.4 %shard_map.129 = (bf16[8192,128]{1,0:T(8,128)(2,1)}, f32[1,32,128]{2,1,0:T(8,128)}, f32[1,32,128]{2,1,0:T(8,128)}, f32[1,32,64]{2,1,0:T(8,128)}, f32[1,32]{1,0:T(1,128)}) custom-call(bf16[8192,128]{1,0:T(8,128)(2,1)S(1)} %get-tuple-element.15.refs_0_, f32[1,32,128]{2,1,0:T(8,128)S(1)} %get-tuple-element.16.refs_1_, ...), custom_call_target="tpu_custom_call" | custom-call | tf_op jit(solution)/shard_map/pallas_call | solution.py:558

commit v4 on v3

--- a/solution.py
+++ b/solution.py
@@ -11,7 +11,7 @@
 LANES = 256
 CHUNKS = 2
 K_TILES = 8
-HEAD_START = 3
+HEAD_START = 0
 F32 = jnp.float32
 BF16 = jnp.bfloat16
 MESH = pl.DeviceIdType.MESH
@@ -57,11 +57,13 @@
 
 
 def silu_pair(half):
-    t = jnp.tanh(half)
-    a = 1.0 + t
-    h = half * a
-    slope = a + h * (1.0 - t)
-    return h, slope
+    a = 1.0 + jnp.tanh(half)
+    return half * a, a
+
+
+def slope_of(gate_ref, act_ref, p):
+    a = gate_ref[p]
+    return a + act_ref[p] * (2.0 - a)
 
 
 def kernel(
@@ -99,6 +101,8 @@
     p2_ref,
     s1_ref,
     s2_ref,
+    f1_ref,
+    f2_ref,
     v_ref,
     sc_ref,
     q_ref,
@@ -217,6 +221,7 @@
         h1, s1 = silu_pair(jnp.dot(x_pair(p), w1f[...], preferred_element_type=F32))
         put_pair(h1_ref, p, h1.astype(BF16))
         s1_ref[p] = s1
+        f1_ref[p] = h1
 
     def turn(p):
         put_turned(h1t_ref, p, pair_of(h1_ref, p))
@@ -226,6 +231,7 @@
         h2, s2 = silu_pair(jnp.dot(pair_of(h1_ref, p), w2f[...], preferred_element_type=F32))
         put_pair(h2_ref, p, h2.astype(BF16))
         s2_ref[p] = s2
+        f2_ref[p] = h2
 
     def heads(p):
         left = []
@@ -358,20 +364,20 @@
 
     def back_two(p):
         h2g = jnp.dot(pair_of(p1_ref, p), wfb[...], preferred_element_type=F32)
-        put_pair(p2_ref, p, (h2g * s2_ref[p]).astype(BF16))
+        put_pair(p2_ref, p, (h2g * slope_of(s2_ref, f2_ref, p)).astype(BF16))
 
     def back_one(p):
         h1g = jnp.dot(pair_of(p2_ref, p), w2b[...], preferred_element_type=F32)
-        put_pair(p1_ref, p, (h1g * s1_ref[p]).astype(BF16))
+        put_pair(p1_ref, p, (h1g * slope_of(s1_ref, f1_ref, p)).astype(BF16))
 
     def finish(p):
         got = jnp.dot(pair_of(p1_ref, p), w1b[...], preferred_element_type=F32).astype(BF16)
         o_ref[pl.ds(p * span, LANES), :] = got[:, :width]
         o_ref[pl.ds(p * span + LANES, LANES), :] = got[:, width:]
 
-    def weight_grad(turned, grads):
+    def weight_grad(turned, grads, ch):
         total = None
-        for t0 in range(0, tiles, K_TILES):
+        for t0 in range(ch * tiles_c, (ch + 1) * tiles_c, K_TILES):
             left = jnp.concatenate(
                 [turned[t] for t in range(t0, t0 + K_TILES)], axis=1
             )
@@ -382,18 +388,21 @@
 
     share = width // n_ray
 
-    def red_copy(d, first):
+    def red_copy(d, m):
         to = lax.rem(my_ray + d, n_ray)
-        part = pl.ds(0, 1) if first else pl.ds(1, 2)
-        sem = d + n_ray * first
         return pltpu.make_async_remote_copy(
-            src_ref=acc.at[part, pl.ds(pl.multiple_of(to * share, share), share), :],
-            dst_ref=red_ref.at[d, part],
-            send_sem=red_send.at[sem],
-            recv_sem=red_recv.at[sem],
+            src_ref=acc.at[pl.ds(m, 1), pl.ds(pl.multiple_of(to * share, share), share), :],
+            dst_ref=red_ref.at[d, pl.ds(m, 1)],
+            send_sem=red_send.at[m * n_ray + d],
+            recv_sem=red_recv.at[m * n_ray + d],
             device_id={"ray": to},
             device_id_type=MESH,
         )
+
+    partners = sorted(range(1, n_ray), key=lambda d: abs(d - n_ray // 2))
+
+    def add_grad(m, value, ch):
+        acc[m] = value if ch == 0 else acc[m] + value
 
     def late_layers(ch):
         first, last = ch * pairs_c, (ch + 1) * pairs_c
@@ -429,42 +438,46 @@
         first, last = ch * pairs_c, (ch + 1) * pairs_c
         composite(ch)
         if ch > 0:
-            for p in range(first - pairs_c, first):
-                back_one(p)
+            add_grad(0, weight_grad(xt_ref, p1_ref, ch - 1), ch - 1)
         for p in range(first, last):
             feature_grads(p)
         for p in range(first, last):
             dens = dens + ray_sums(p)
         for p in range(first, last):
             back_two(p)
+        if ch < CHUNKS - 1:
+            for p in range(first, last):
+                back_one(p)
+            add_grad(1, weight_grad(h1t_ref, p2_ref, ch), ch)
+    u_hi, u_low = split_two(u_ref[...])
+    s_hi, s_low = split_two(sc_ref[...])
+    left = jnp.concatenate([u_hi, u_hi, u_low, *split_three(dens)], axis=0)
+    right = jnp.concatenate([s_hi, s_low, s_hi, unit, unit, unit], axis=0)
+    acc[2] = contract_rows(left.astype(BF16), right.astype(BF16))
+    add_grad(1, weight_grad(h1t_ref, p2_ref, CHUNKS - 1), CHUNKS - 1)
+    for d in partners:
+        red_copy(d, 1).start()
+        red_copy(d, 2).start()
     for p in range(pairs - pairs_c, pairs):
         back_one(p)
-    acc[1] = weight_grad(h1t_ref, p2_ref)
-    u_hi, u_low = split_two(u_ref[...])
-    s_hi, s_low = split_two(sc_ref[...])
-    parts = split_three(dens)
-    acc[2] = contract_rows(
-        jnp.concatenate([u_hi, u_hi, u_low, *parts], axis=0).astype(BF16),
-        jnp.concatenate([s_hi, s_low, s_hi, unit, unit, unit], axis=0).astype(BF16),
-    )
-    for d in range(1, n_ray):
+    add_grad(0, weight_grad(xt_ref, p1_ref, CHUNKS - 1), CHUNKS - 1)
+    for d in partners:
         red_copy(d, 0).start()
-    acc[0] = weight_grad(xt_ref, p1_ref)
-    for d in range(1, n_ray):
-        red_copy(d, 1).start()
     for p in range(pairs):
         finish(p)
 
-    total = acc[:, pl.ds(pl.multiple_of(my_ray * share, share), share), :]
-    for d in range(1, n_ray):
-        red_copy(d, 0).wait()
-        red_copy(d, 1).wait()
-        total = total + red_ref[d]
-    total = total * (1.0 / LOSS_SCALE)
-    g1_ref[0] = total[0]
-    g2_ref[0] = total[1]
-    g3_ref[0] = total[2][:, :feat]
-    g4_ref[...] = total[2].T[feat : feat + 1, :]
+    def reduced(m):
+        total = acc[m, pl.ds(pl.multiple_of(my_ray * share, share), share), :]
+        for d in partners:
+            red_copy(d, m).wait()
+            total = total + red_ref[d, m]
+        return total * (1.0 / LOSS_SCALE)
+
+    both = reduced(2)
+    g3_ref[0] = both[:, :feat]
+    g4_ref[...] = both.T[feat : feat + 1, :]
+    g2_ref[0] = reduced(1)
+    g1_ref[0] = reduced(0)
 
 
 def hand_out(*refs):
@@ -519,6 +532,8 @@
                 pltpu.VMEM(tile_shape, BF16),
                 pltpu.VMEM((pairs, LANES, 2 * width), F32),
                 pltpu.VMEM((pairs, LANES, 2 * width), F32),
+                pltpu.VMEM((pairs, LANES, 2 * width), F32),
+                pltpu.VMEM((pairs, LANES, 2 * width), F32),
                 pltpu.VMEM((rays, width), F32),
                 pltpu.VMEM((rays, width), F32),
                 pltpu.VMEM((tiles, LANES), F32),
@@ -538,8 +553,8 @@
                 pltpu.SemaphoreType.DMA((CHUNKS,)),
                 pltpu.SemaphoreType.DMA((CHUNKS, n_brick)),
                 pltpu.SemaphoreType.DMA((CHUNKS, n_brick)),
-                pltpu.SemaphoreType.DMA((2 * n_ray,)),
-                pltpu.SemaphoreType.DMA((2 * n_ray,)),
+                pltpu.SemaphoreType.DMA((3 * n_ray,)),
+                pltpu.SemaphoreType.DMA((3 * n_ray,)),
             ],
             compiler_params=pltpu.CompilerParams(
                 collective_id=0, has_side_effects=True, vmem_limit_bytes=52 * 1024 * 1024

time: 20.6 us -> 20.1 us (0.976)
  Pallas kernels: 19.8 us -> 19.3 us
    pallas_call x1, Pallas kernels: 18.4 us -> 17.9 us  [shards(): pl.pallas_call(functools.partial(kernel, n_brick, n_ray, per_ray), out_sh...]
where the time goes in v4:
time: 20.1 us; the launch traced here: 20 us
  Pallas kernels  19.3 us (96%)
  between operations  0.64 us (3%)
    pallas_call x1, Pallas kernels, shards(): pl.pallas_call(functools.partial(kernel, n_brick, n_ray, per_ray), out_sh...  17.9 us
    pallas_call x1, Pallas kernels, shards(): pl.pallas_call(hand_out, out_shape=tuple((jax.ShapeDtypeStruct(o.shape, o...  1.37 us

profile of v4, /device:TPU:0, one launch (start us, length us, event | category | flops | bytes accessed | tf_op | source)
XLA Modules:
  0.0 20.0 jit_solution(14543608548950257324)
XLA Ops:
  0.6 17.9 %shard_map.128 = (bf16[8192,128]{1,0:T(8,128)(2,1)S(1)}, f32[1,32,128]{2,1,0:T(8,128)S(1)}, f32[1,32,128]{2,1,0:T(8,128)S(1)}, f32[1,32,64]{2,1,0:T(8,128)S(1)}, f32[1,32]{1,0:T(1,128)S(1)}) custom-call(bf16[8192,128]{1,0:T(8,128)(2,1)} %bitcast.8, s32[1,256]{1,0:T(1,128)} %bitcast.10, f32[1,256]{1,0:T(1,128)} %bitcast.11, s32[1,256]{1,0:T(1,128)} %bitcast.12, ...), custom_call_target="tpu_custom_call" | custom-call | tf_op jit(solution)/shard_map/pallas_call | solution.py:506
  18.6 1.4 %shard_map.129 = (bf16[8192,128]{1,0:T(8,128)(2,1)}, f32[1,32,128]{2,1,0:T(8,128)}, f32[1,32,128]{2,1,0:T(8,128)}, f32[1,32,64]{2,1,0:T(8,128)}, f32[1,32]{1,0:T(1,128)}) custom-call(bf16[8192,128]{1,0:T(8,128)(2,1)S(1)} %get-tuple-element.15.refs_0_, f32[1,32,128]{2,1,0:T(8,128)S(1)} %get-tuple-element.16.refs_1_, ...), custom_call_target="tpu_custom_call" | custom-call | tf_op jit(solution)/shard_map/pallas_call | solution.py:573

commit v5 on v4

--- a/solution.py
+++ b/solution.py
@@ -10,8 +10,9 @@
 LOSS_SCALE = 1024.0
 LANES = 256
 CHUNKS = 2
-K_TILES = 8
+K_TILES = 16
 HEAD_START = 0
+EARLY_PAIRS = 2
 F32 = jnp.float32
 BF16 = jnp.bfloat16
 MESH = pl.DeviceIdType.MESH
@@ -102,7 +103,6 @@
     s1_ref,
     s2_ref,
     f1_ref,
-    f2_ref,
     v_ref,
     sc_ref,
     q_ref,
@@ -148,12 +148,13 @@
             )
         )
     ]
-    piece = rows // CHUNKS
+    chunk_rows = rows // CHUNKS
+    cuts = [0, EARLY_PAIRS * span] + [(i + 1) * chunk_rows for i in range(CHUNKS)]
     pieces = [
         pltpu.make_async_copy(
-            x_hbm.at[pl.ds(i * piece, piece)], x_ref.at[pl.ds(i * piece, piece)], x_sem.at[i]
-        )
-        for i in range(CHUNKS)
+            x_hbm.at[pl.ds(lo, hi - lo)], x_ref.at[pl.ds(lo, hi - lo)], x_sem.at[i]
+        )
+        for i, (lo, hi) in enumerate(zip(cuts, cuts[1:]))
     ]
     small[0].start()
     pieces[0].start()
@@ -196,7 +197,7 @@
             for i in range(len(sample_values))
         ]
 
-    for copy in small:
+    for copy in small + pieces[:1]:
         copy.wait()
     w1 = w1_ref[0].astype(F32)
     w1f[...] = block_diag(w1 * 0.5).astype(BF16)
@@ -230,8 +231,7 @@
     def second_layer(p):
         h2, s2 = silu_pair(jnp.dot(pair_of(h1_ref, p), w2f[...], preferred_element_type=F32))
         put_pair(h2_ref, p, h2.astype(BF16))
-        s2_ref[p] = s2
-        f2_ref[p] = h2
+        s2_ref[p] = s2 + h2 * (2.0 - s2)
 
     def heads(p):
         left = []
@@ -364,7 +364,7 @@
 
     def back_two(p):
         h2g = jnp.dot(pair_of(p1_ref, p), wfb[...], preferred_element_type=F32)
-        put_pair(p2_ref, p, (h2g * slope_of(s2_ref, f2_ref, p)).astype(BF16))
+        put_pair(p2_ref, p, (h2g * s2_ref[p]).astype(BF16))
 
     def back_one(p):
         h1g = jnp.dot(pair_of(p2_ref, p), w2b[...], preferred_element_type=F32)
@@ -414,13 +414,15 @@
                 if k >= first:
                     heads(k)
 
-    pieces[0].wait()
-    for p in range(pairs_c):
+    for p in range(EARLY_PAIRS):
+        first_layer(p)
+    pieces[1].wait()
+    for p in range(EARLY_PAIRS, pairs_c):
         first_layer(p)
     late_layers(0)
     for ch in range(1, CHUNKS):
         first = ch * pairs_c
-        pieces[ch].wait()
+        pieces[ch + 1].wait()
         middle(ch - 1)
         for p in range(first, first + HEAD_START):
             first_layer(p)
@@ -533,7 +535,6 @@
                 pltpu.VMEM((pairs, LANES, 2 * width), F32),
                 pltpu.VMEM((pairs, LANES, 2 * width), F32),
                 pltpu.VMEM((pairs, LANES, 2 * width), F32),
-                pltpu.VMEM((pairs, LANES, 2 * width), F32),
                 pltpu.VMEM((rays, width), F32),
                 pltpu.VMEM((rays, width), F32),
                 pltpu.VMEM((tiles, LANES), F32),
@@ -550,7 +551,7 @@
                 pltpu.VMEM((CHUNKS, n_brick, 8, rays // CHUNKS), F32),
                 pltpu.VMEM((n_ray, 3, share, width), F32),
                 pltpu.SemaphoreType.DMA((8,)),
-                pltpu.SemaphoreType.DMA((CHUNKS,)),
+                pltpu.SemaphoreType.DMA((CHUNKS + 1,)),
                 pltpu.SemaphoreType.DMA((CHUNKS, n_brick)),
                 pltpu.SemaphoreType.DMA((CHUNKS, n_brick)),
                 pltpu.SemaphoreType.DMA((3 * n_ray,)),

time: 20.1 us -> 19.9 us (0.990)
    pallas_call x1, Pallas kernels: 17.9 us -> 17.7 us  [shards(): pl.pallas_call(functools.partial(kernel, n_brick, n_ray, per_ray), out_sh...]
where the time goes in v5:
time: 19.9 us; the launch traced here: 19.7 us
  Pallas kernels  19.1 us (96%)
  between operations  0.64 us (3%)
    pallas_call x1, Pallas kernels, shards(): pl.pallas_call(functools.partial(kernel, n_brick, n_ray, per_ray), out_sh...  17.7 us
    pallas_call x1, Pallas kernels, shards(): pl.pallas_call(hand_out, out_shape=tuple((jax.ShapeDtypeStruct(o.shape, o...  1.37 us

profile of v5, /device:TPU:0, one launch (start us, length us, event | category | flops | bytes accessed | tf_op | source)
XLA Modules:
  0.0 19.7 jit_solution(17708686146781593924)
XLA Ops:
  0.6 17.7 %shard_map.128 = (bf16[8192,128]{1,0:T(8,128)(2,1)S(1)}, f32[1,32,128]{2,1,0:T(8,128)S(1)}, f32[1,32,128]{2,1,0:T(8,128)S(1)}, f32[1,32,64]{2,1,0:T(8,128)S(1)}, f32[1,32]{1,0:T(1,128)S(1)}) custom-call(bf16[8192,128]{1,0:T(8,128)(2,1)} %bitcast.8, s32[1,256]{1,0:T(1,128)} %bitcast.10, f32[1,256]{1,0:T(1,128)} %bitcast.11, s32[1,256]{1,0:T(1,128)} %bitcast.12, ...), custom_call_target="tpu_custom_call" | custom-call | tf_op jit(solution)/shard_map/pallas_call | solution.py:508
  18.3 1.4 %shard_map.129 = (bf16[8192,128]{1,0:T(8,128)(2,1)}, f32[1,32,128]{2,1,0:T(8,128)}, f32[1,32,128]{2,1,0:T(8,128)}, f32[1,32,64]{2,1,0:T(8,128)}, f32[1,32]{1,0:T(1,128)}) custom-call(bf16[8192,128]{1,0:T(8,128)(2,1)S(1)} %get-tuple-element.15.refs_0_, f32[1,32,128]{2,1,0:T(8,128)S(1)} %get-tuple-element.16.refs_1_, ...), custom_call_target="tpu_custom_call" | custom-call | tf_op jit(solution)/shard_map/pallas_call | solution.py:574
